TPU v7x, 256 devices: a whole 4x4x8 slice. The times are simulated.
256 devices in a mesh: row: 8 (over y, z_hi), col: 32 (over z_lo, x, core).
Axes of the slice: x: 4, y: 4, z: 8 (z_hi: 2, z_lo: 4; z = z_hi * 4 + z_lo), core: 2. Of those that a mesh axis runs over, the one named last changes fastest.
Arguments:
- transfer: bfloat16 [2, 4096, 16384], P(None, 'row', 'col'), may hold values from -0.046875 to 0.046875
- phase: float32 [16384, 128], P('col', 'row'), may hold values from -3.140625 to 3.140625
- trap_index: int32 [128, 64], replicated, may hold values from 0 to 4095
- levels: int32 [128, 64], replicated, may hold values from 1 to 4
- weights_old: float32 [128, 64], replicated, may hold values from 0.5 to 1.5
Outputs:
- far_field: bfloat16 [4096, 2, 128], P(('row', 'col'))
- weights_new: float32 [128, 64], replicated
- slm_field: float32 [16384, 2, 128], P('col', None, 'row')
All inputs are finite; a program needn't handle non-finite values.
Results may differ from a plain program's by a relative error of at most 0.013.
Values may be sent and summed in bfloat16 or wider, within the bound.
A program may use at most 64 MiB of HBM per device.

v0:
```python
import jax
import jax.numpy as jnp
from jax import lax
from jax.sharding import PartitionSpec as P

MODES = 16384
TRAPS = 64


def back_terms(transfer, piece):
    count = piece.shape[2]
    real_rows = transfer[0]
    imag_rows = transfer[1]
    stacked = jnp.concatenate([piece[:, 0], piece[:, 1]], axis=1)
    dims = (((0,), (0,)), ((), ()))
    first_b = lax.dot_general(real_rows, stacked, dims, preferred_element_type=jnp.float32)
    second_b = lax.dot_general(imag_rows, stacked, dims, preferred_element_type=jnp.float32)
    part = jnp.concatenate(
        [first_b[:, :count] + second_b[:, count:], first_b[:, count:] - second_b[:, :count]], axis=1
    )
    return part


def trap_lookup(block, trap_index, offset):
    count = block.shape[2]
    height = block.shape[0]
    local = trap_index - offset
    inside = (local >= 0) & (local < height)
    clipped = jnp.clip(local, 0, height - 1)
    pattern_ids = jnp.arange(count, dtype=jnp.int32)[:, None]
    values = block[clipped, :, pattern_ids]
    return (inside, clipped, pattern_ids, values)


def body(transfer, phase, trap_index, levels, weights_old):
    n_col = lax.axis_size("col")
    tile_rows = transfer.shape[1]
    pix_rows = tile_rows // n_col
    modes_local = transfer.shape[2]
    field = jnp.stack([jnp.cos(phase), jnp.sin(phase)], axis=0).astype(jnp.bfloat16)
    whole = lax.all_gather(field, "row", axis=2, tiled=True)
    count = whole.shape[2]
    joined = jnp.concatenate([whole[0], whole[1]], axis=1)
    target = levels.astype(jnp.float32)
    row_start = lax.axis_index("row") * tile_rows
    real_rows = transfer[0]
    imag_rows = transfer[1]
    first = jnp.dot(real_rows, joined, preferred_element_type=jnp.float32)
    second = jnp.dot(imag_rows, joined, preferred_element_type=jnp.float32)
    mine = lax.psum_scatter(
        jnp.stack(
            [first[:, :count] - second[:, count:], first[:, count:] + second[:, :count]], axis=1
        ),
        "col",
        scatter_dimension=0,
        tiled=True,
    )
    far_field = mine.astype(jnp.bfloat16)
    offset = row_start + lax.axis_index("col") * pix_rows
    inside, clipped, pattern_ids, values = trap_lookup(mine, trap_index, offset)
    amp_local = jnp.sqrt(values[..., 0] ** 2 + values[..., 1] ** 2 + 0.25)
    amp = lax.psum(jnp.where(inside, amp_local, 0.0), ("row", "col"))
    ratio = amp / target
    weights_new = weights_old * jnp.mean(ratio, axis=1, keepdims=True) / ratio
    coef = weights_new * target / amp
    adds = jnp.where(inside[..., None], coef[..., None] * values, 0.0)
    projected = (
        jnp.zeros(mine.shape, jnp.float32)
        .at[clipped, :, pattern_ids]
        .add(adds)
        .astype(jnp.bfloat16)
    )
    total = back_terms(transfer, lax.all_gather(projected, "col", axis=0, tiled=True))
    back = total.reshape(modes_local, 2, count)
    back = lax.psum_scatter(
        back.astype(jnp.bfloat16), "row", scatter_dimension=2, tiled=True
    ).astype(jnp.float32)
    scaled = jnp.sqrt(jnp.float32(MODES) / jnp.float32(TRAPS)) * back
    slm_field = scaled / jnp.sqrt(scaled[:, 0:1] ** 2 + scaled[:, 1:2] ** 2 + 1.0)
    return (far_field, weights_new, slm_field)


def solution(mesh):
    placed = (P(None, "row", "col"), P("col", "row"), P(), P(), P())
    return jax.shard_map(
        body,
        mesh=mesh,
        in_specs=placed,
        out_specs=(P(("row", "col"), None, None), P(), P("col", None, "row")),
        check_vma=False,
    )
```

profile of v0, /device:TPU:2, one launch (start us, length us, event | category | flops | bytes accessed | tf_op | source)
XLA Modules:
  0.0 716.5 jit_solution(8957432366630390848)
XLA Ops:
  7.2 0.9 fusion.20
  8.2 46.2 %all_gather.6 = bf16[2,512,128]{1,2,0:T(8,128)(2,1)S(1)} all-gather(bf16[2,512,16]{1,2,0:T(8,128)(2,1)S(1)} %pad_maximum_fusion.8), channel_id=1, replica_groups=mesh['row'=8,'col'=32] {'row'}, dimensions={2}, use_global_device_ids=true | all-gather | bytes 294912 | tf_op jit(solution)/shard_map/all_gather | solution.py:41
  54.3 1.4 convolution_bitcast_fusion.2
  55.7 1.4 convolution_bitcast_fusion.3
  57.2 1.0 copy.31
  58.9 0.6 dynamic-slice
  60.1 273.9 %all-reduce.3.cloned.1.call-done = f32[512,2,128]{2,1,0:T(2,128)} async-done(((f32[512,2,128]{2,1,0:T(2,128)}), f32[512,2,128]{2,1,0:T(2,128)}) %all-reduce.3.cloned.1.call-update) | async-done | bytes 524304
  334.0 1.3 fusion.27
  335.3 0.4 copy.33
  335.7 88.8 %gather_fusion = f32[8192,2]{1,0:T(8,128)} fusion(f32[16,2,128]{1,2,0:T(8,128)S(1)} %copy.33, s32[8192]{0:T(1024)S(1)} %reshape.27), kind=kCustom, calls=%fused_computation | custom fusion | bytes 196608 | tf_op jit(solution)/shard_map/gather | solution.py:31
  424.5 8.0 %fusion.28 = (f32[128,64,1]{2,1,0:T(8,128)}, f32[128,64,1]{2,1,0:T(8,128)}) fusion(f32[128,64,2]{2,1,0:T(8,128)} %bitcast.49), kind=kLoop, calls=%fused_computation.66 | loop fusion | bytes 131072 | tf_op jit(solution)/shard_map/slice | solution.py:61
  432.5 3.8 copy.40
  436.3 3.7 copy.41
  440.0 81.6 %psum.7 = f32[128,64]{0,1:T(8,128)S(1)} all-reduce(f32[128,64]{0,1:T(8,128)S(1)} %get-tuple-element.14), channel_id=1, replica_groups=mesh['row'=8,'col'=32] {'row','col'}, use_global_device_ids=true, to_apply=%region_1.2 | all-reduce | flops 8192 | bytes 65536 | tf_op jit(solution)/shard_map/psum | solution.py:62
  521.8 0.6 multiply_divide_fusion
  522.6 7.7 %multiply_select_fusion = f32[128,64,2]{2,1,0:T(8,128)} fusion(f32[128,64,2]{2,1,0:T(8,128)} %bitcast.50, f32[128,64]{1,0:T(8,128)S(1)} %copy.38, pred[128,64]{1,0:T(8,128)(4,1)S(1)} %copy.37), kind=kLoop, calls=%fused_computation.2 | loop fusion | flops 32768 | bytes 172032 | tf_op jit(solution)/shard_map/jit(_where)/select_n | solution.py:66
  530.3 56.4 %scatter_custom_fusion = f32[2048,2]{1,0:T(8,128)S(1)} fusion(s32[8192]{0:T(1024)S(1)} %reshape.33, f32[8192,2]{1,0:T(8,128)} %bitcast.51, f32[]{:T(128)} %constant.8.clone.1), kind=kCustom, calls=%fused_computation.12 | custom fusion | flops 16384 | bytes 16896
  587.0 41.1 %all_gather.7 = bf16[512,2,128]{2,0,1:T(8,128)(2,1)S(1)} all-gather(bf16[16,2,128]{2,0,1:T(8,128)(2,1)S(1)} %bitcast.54), channel_id=1, replica_groups=mesh['row'=8,'col'=32] {'col'}, dimensions={0}, use_global_device_ids=true | all-gather | bytes 270336 | tf_op jit(solution)/shard_map/all_gather | solution.py:73
  628.2 0.3 convolution_bitcast_fusion
  628.5 0.3 convolution_bitcast_fusion.1
  628.9 0.7 pad_maximum_fusion.3
  629.7 77.9 %reduce-scatter.2.cloned.1.call-done = bf16[512,2,16]{0,2,1:T(8,128)(2,1)} async-done(((bf16[512,2,128]{0,2,1:T(8,128)(2,1)}), bf16[512,2,16]{0,2,1:T(8,128)(2,1)}) %reduce-scatter.2.cloned.1.call-update) | async-done | bytes 32784 | tf_op jit(solution)/shard_map/reduce_scatter | solution.py:75
  707.5 0.8 convert_multiply_fusion
  708.3 1.4 broadcast_divide_fusion
  (41 shorter events, 1.5 us)
Async XLA Ops:
  7.2 51.2 %copy-start.5 = (s32[2]{0:T(128)S(1)}, s32[2]{0:T(128)}, u32[]{:S(2)}) copy-start(s32[2]{0:T(128)} %constant.34) | copy-start | bytes 28
  7.2 51.3 %copy-start.4 = (s32[2]{0:T(128)S(1)}, s32[2]{0:T(128)}, u32[]{:S(2)}) copy-start(s32[2]{0:T(128)} %constant.37) | copy-start | bytes 28
  7.2 51.1 %copy-start.1 = (s32[128,64]{0,1:T(8,128)S(1)}, s32[128,64]{0,1:T(8,128)}, u32[]{:S(2)}) copy-start(s32[128,64]{0,1:T(8,128)} %param.7) | copy-start | bytes 98308
  7.2 326.8 %all-reduce.3.cloned.1.call-start = ((), (), s32[]{:S(2)}) async-start(), calls=%async_computation.2 | async-start | bytes 1048576
  8.1 50.8 %copy-start.6 = (u32[256]{0:T(256)S(1)}, u32[256]{0:T(256)}, u32[]{:S(2)}) copy-start(u32[256]{0:T(256)} %constant.57) | copy-start | bytes 3076
  58.2 649.3 %reduce-scatter.2.cloned.1.call-start = ((), (), s32[]{:S(2)}) async-start(), calls=%async_computation.1 | async-start | bytes 294912 | tf_op jit(solution)/shard_map/reduce_scatter | solution.py:75
  432.5 89.2 %copy-start.2 = (s32[128,64]{0,1:T(8,128)S(1)}, s32[128,64]{0,1:T(8,128)}, u32[]{:S(2)}) copy-start(s32[128,64]{0,1:T(8,128)} %param.8) | copy-start | bytes 98308
  432.5 89.3 %copy-start.3 = (f32[128,64]{0,1:T(8,128)S(1)}, f32[128,64]{0,1:T(8,128)}, u32[]{:S(2)}) copy-start(f32[128,64]{0,1:T(8,128)} %param.9) | copy-start | bytes 98308
  522.6 105.6 %copy-start = (bf16[2,512,512]{2,1,0:T(8,128)(2,1)S(1)}, bf16[2,512,512]{2,1,0:T(8,128)(2,1)}, u32[]{:S(2)}) copy-start(bf16[2,512,512]{2,1,0:T(8,128)(2,1)} %param.5) | copy-start | bytes 3145732
Sparse Core Ops, SparseCore 0:
  58.4 275.5 all-reduce.2
  629.8 77.6 reduce-scatter.1
where the time goes:
time: 717 us
  waiting for transfers between devices  352 us (49%)
  blocking collectives  169 us (24%)
  local copies, waits for them, and re-layouts  107 us (15%)
  other arithmetic  70.4 us (10%)
  between operations  14.9 us (2%)
    unnamed x3, waiting for transfers between devices  274 us
    gather x1, local copies, waits for them, and re-layouts, trap_lookup(): values = block[clipped, :, pattern_ids]  88.8 us
    psum x1, blocking collectives, body(): amp = lax.psum(jnp.where(inside, amp_local, 0.0), ('row', 'col'))  81.6 us
    reduce_scatter x1, waiting for transfers between devices, body(): lax.psum_scatter(back.astype(jnp.bfloat16), 'row', scatter_dimension=2, t...  77.9 us
    unnamed x4, other arithmetic  56.5 us
    all_gather x1, blocking collectives, body(): whole = lax.all_gather(field, 'row', axis=2, tiled=True)  46.2 us
    all_gather x1, blocking collectives, body(): lax.all_gather(projected, 'col', axis=0, tiled=True)  41.1 us
  transfers between devices with their start and end apart: 2, of which 2 were waited for; matrix products, arithmetic and copies ran while one was open for 0% of the time, Pallas kernels for 0%

commit v1 on v0

--- a/solution.py
+++ b/solution.py
@@ -70,7 +70,12 @@
         .add(adds)
         .astype(jnp.bfloat16)
     )
-    total = back_terms(transfer, lax.all_gather(projected, "col", axis=0, tiled=True))
+    total = back_terms(
+        transfer,
+        jnp.concatenate(
+            lax.all_to_all(jnp.stack([projected] * lax.axis_size("col")), "col", 0, 0), axis=0
+        ),
+    )
     back = total.reshape(modes_local, 2, count)
     back = lax.psum_scatter(
         back.astype(jnp.bfloat16), "row", scatter_dimension=2, tiled=True

time: 717 us -> 692 us (0.965)
  blocking collectives: 169 us -> 143 us
    all_gather x1 -> x0, blocking collectives: 41.1 us -> none  [body(): lax.all_gather(projected, 'col', axis=0, tiled=True)]
    all_to_all x0 -> x1, blocking collectives: none -> 15 us  [body(): lax.all_to_all(jnp.stack([projected] * lax.axis_size('col')), 'col', 0, 0)]
where the time goes in v1:
time: 692 us
  waiting for transfers between devices  353 us (51%)
  blocking collectives  143 us (21%)
  local copies, waits for them, and re-layouts  107 us (15%)
  other arithmetic  70.4 us (10%)
  between operations  14.9 us (2%)
    unnamed x3, waiting for transfers between devices  274 us
    gather x1, local copies, waits for them, and re-layouts, trap_lookup(): values = block[clipped, :, pattern_ids]  88.8 us
    psum x1, blocking collectives, body(): amp = lax.psum(jnp.where(inside, amp_local, 0.0), ('row', 'col'))  81.6 us
    reduce_scatter x1, waiting for transfers between devices, body(): lax.psum_scatter(back.astype(jnp.bfloat16), 'row', scatter_dimension=2, t...  79 us
    unnamed x4, other arithmetic  56.6 us
    all_gather x1, blocking collectives, body(): whole = lax.all_gather(field, 'row', axis=2, tiled=True)  46.2 us
    all_to_all x1, blocking collectives, body(): lax.all_to_all(jnp.stack([projected] * lax.axis_size('col')), 'col', 0, 0)  15 us
  transfers between devices with their start and end apart: 2, of which 2 were waited for; matrix products, arithmetic and copies ran while one was open for 0% of the time, Pallas kernels for 0%

profile of v1, /device:TPU:2, one launch (start us, length us, event | category | flops | bytes accessed | tf_op | source)
XLA Modules:
  0.0 691.6 jit_solution(10233618889842682017)
XLA Ops:
  7.2 0.9 fusion.20
  8.2 46.2 %all_gather.3 = bf16[2,512,128]{1,2,0:T(8,128)(2,1)S(1)} all-gather(bf16[2,512,16]{1,2,0:T(8,128)(2,1)S(1)} %pad_maximum_fusion.8), channel_id=1, replica_groups=mesh['row'=8,'col'=32] {'row'}, dimensions={2}, use_global_device_ids=true | all-gather | bytes 294912 | tf_op jit(solution)/shard_map/all_gather | solution.py:41
  54.3 1.4 convolution_bitcast_fusion.2
  55.7 1.4 convolution_bitcast_fusion.3
  57.2 1.0 copy.31
  58.9 0.6 dynamic-slice
  60.1 273.9 %all-reduce.3.cloned.1.call-done = f32[512,2,128]{2,1,0:T(2,128)} async-done(((f32[512,2,128]{2,1,0:T(2,128)}), f32[512,2,128]{2,1,0:T(2,128)}) %all-reduce.3.cloned.1.call-update) | async-done | bytes 524304
  334.0 1.3 fusion.27
  335.3 0.4 copy.33
  335.7 88.8 %gather_fusion = f32[8192,2]{1,0:T(8,128)} fusion(f32[16,2,128]{1,2,0:T(8,128)S(1)} %copy.33, s32[8192]{0:T(1024)S(1)} %reshape.33), kind=kCustom, calls=%fused_computation | custom fusion | bytes 196608 | tf_op jit(solution)/shard_map/gather | solution.py:31
  424.5 8.0 %fusion.28 = (f32[128,64,1]{2,1,0:T(8,128)}, f32[128,64,1]{2,1,0:T(8,128)}) fusion(f32[128,64,2]{2,1,0:T(8,128)} %bitcast.51), kind=kLoop, calls=%fused_computation.66 | loop fusion | bytes 131072 | tf_op jit(solution)/shard_map/slice | solution.py:61
  432.5 3.8 copy.41
  436.3 3.7 copy.42
  440.0 81.6 %psum.7 = f32[128,64]{0,1:T(8,128)S(1)} all-reduce(f32[128,64]{0,1:T(8,128)S(1)} %get-tuple-element.14), channel_id=1, replica_groups=mesh['row'=8,'col'=32] {'row','col'}, use_global_device_ids=true, to_apply=%region_1.2 | all-reduce | flops 8192 | bytes 65536 | tf_op jit(solution)/shard_map/psum | solution.py:62
  521.8 0.6 multiply_divide_fusion
  522.6 7.7 %multiply_select_fusion = f32[128,64,2]{2,1,0:T(8,128)} fusion(f32[128,64,2]{2,1,0:T(8,128)} %bitcast.52, f32[128,64]{1,0:T(8,128)S(1)} %copy.38, pred[128,64]{1,0:T(8,128)(4,1)S(1)} %copy.37), kind=kLoop, calls=%fused_computation.2 | loop fusion | flops 32768 | bytes 172032 | tf_op jit(solution)/shard_map/jit(_where)/select_n | solution.py:66
  530.2 56.4 %scatter_custom_fusion = f32[2048,2]{1,0:T(8,128)S(1)} fusion(s32[8192]{0:T(1024)S(1)} %reshape.39, f32[8192,2]{1,0:T(8,128)} %bitcast.53, f32[]{:T(128)} %constant.8.clone.1), kind=kCustom, calls=%fused_computation.12 | custom fusion | flops 16384 | bytes 16896
  587.0 15.0 %all_to_all.5 = bf16[32,16,2,128]{3,1,2,0:T(8,128)(2,1)S(1)} all-to-all(bf16[32,16,2,128]{3,1,2,0:T(8,128)(2,1)S(1)} %stack.23), channel_id=1, replica_groups=mesh['row'=8,'col'=32] {'col'}, dimensions={0} | all-to-all | bytes 524288 | tf_op jit(solution)/shard_map/all_to_all | solution.py:76
  602.1 0.3 convolution_bitcast_fusion
  602.4 0.3 convolution_bitcast_fusion.1
  602.9 0.7 pad_maximum_fusion.3
  603.6 79.0 %reduce-scatter.2.cloned.1.call-done = bf16[512,2,16]{0,2,1:T(8,128)(2,1)} async-done(((bf16[512,2,128]{0,2,1:T(8,128)(2,1)}), bf16[512,2,16]{0,2,1:T(8,128)(2,1)}) %reduce-scatter.2.cloned.1.call-update) | async-done | bytes 32784 | tf_op jit(solution)/shard_map/reduce_scatter | solution.py:80
  682.6 0.8 convert_multiply_fusion
  683.4 1.4 broadcast_divide_fusion
  (43 shorter events, 1.6 us)
Async XLA Ops:
  7.2 51.2 %copy-start.5 = (s32[2]{0:T(128)S(1)}, s32[2]{0:T(128)}, u32[]{:S(2)}) copy-start(s32[2]{0:T(128)} %constant.34) | copy-start | bytes 28
  7.2 51.3 %copy-start.4 = (s32[2]{0:T(128)S(1)}, s32[2]{0:T(128)}, u32[]{:S(2)}) copy-start(s32[2]{0:T(128)} %constant.37) | copy-start | bytes 28
  7.2 51.1 %copy-start.1 = (s32[128,64]{0,1:T(8,128)S(1)}, s32[128,64]{0,1:T(8,128)}, u32[]{:S(2)}) copy-start(s32[128,64]{0,1:T(8,128)} %param.7) | copy-start | bytes 98308
  7.2 326.8 %all-reduce.3.cloned.1.call-start = ((), (), s32[]{:S(2)}) async-start(), calls=%async_computation.3 | async-start | bytes 1048576
  8.1 50.8 %copy-start.6 = (u32[256]{0:T(256)S(1)}, u32[256]{0:T(256)}, u32[]{:S(2)}) copy-start(u32[256]{0:T(256)} %constant.57) | copy-start | bytes 3076
  58.2 624.4 %reduce-scatter.2.cloned.1.call-start = ((), (), s32[]{:S(2)}) async-start(), calls=%async_computation.2 | async-start | bytes 294912 | tf_op jit(solution)/shard_map/reduce_scatter | solution.py:80
  432.5 89.2 %copy-start.2 = (s32[128,64]{0,1:T(8,128)S(1)}, s32[128,64]{0,1:T(8,128)}, u32[]{:S(2)}) copy-start(s32[128,64]{0,1:T(8,128)} %param.8) | copy-start | bytes 98308
  432.5 89.3 %copy-start.3 = (f32[128,64]{0,1:T(8,128)S(1)}, f32[128,64]{0,1:T(8,128)}, u32[]{:S(2)}) copy-start(f32[128,64]{0,1:T(8,128)} %param.9) | copy-start | bytes 98308
  530.2 71.9 %copy-start = (bf16[2,512,512]{2,1,0:T(8,128)(2,1)S(1)}, bf16[2,512,512]{2,1,0:T(8,128)(2,1)}, u32[]{:S(2)}) copy-start(bf16[2,512,512]{2,1,0:T(8,128)(2,1)} %param.5) | copy-start | bytes 3145732
Sparse Core Ops, SparseCore 0:
  58.4 275.5 all-reduce.2
  603.7 78.8 reduce-scatter.1
